TPU v7x, 256 devices: a whole 4x4x8 slice. The times are simulated.
256 devices in a mesh: ctx: 128 (over z, x, y_lo, core), head: 2 (over y_hi).
Axes of the slice: x: 4, y: 4 (y_hi: 2, y_lo: 2; y = y_hi * 2 + y_lo), z: 8, core: 2. Of those that a mesh axis runs over, the one named last changes fastest.
Arguments:
- queries: bfloat16 [16384, 2048], P('ctx', 'head'), may hold values from -12 to 12
- barred_key_rows: bfloat16 [16384, 512], P('ctx', 'head'), may hold values from -5.5 to 5.5
- barred_value_rows: bfloat16 [16384, 512], P('ctx', 'head'), may hold values from -12 to 12
- doc_start: int32 [16384], P('ctx'), may hold values from 0 to 16383, as said below
- out_weight: bfloat16 [2048, 4096], P('head'), may hold values from -0.5 to 0.5
Outputs:
- mixed: bfloat16 [16384, 4096], P('ctx', 'head')
Inputs may be any that keep to these rules, and one draw needn't show every extreme that they name: Documents are runs of consecutive positions starting at position 0; the first has exactly 8192 tokens, each other has 2048 to 8192 tokens except the last two: the final position 16383 is a document of one token, and the one before it may be shorter; doc_start of a row is the first position of its document, so it is at most pos of that row.
All inputs are finite; a program needn't handle non-finite values.
Results may differ from a plain program's by a relative error of at most 0.015.
Values may be sent and summed in bfloat16 or wider, within the bound.
A program may use at most 128 MiB of HBM per device.

v0:
```python
import math
import jax
import jax.numpy as jnp
from jax import lax
from jax.sharding import PartitionSpec as P

HEAD_SIZE = 128
STRIPE = 64
MASKED_SCORE = -1e30


def positions(row_index, tok_dev, cycle_size):
    shard_index = row_index // tok_dev
    within = row_index % tok_dev
    return (within // STRIPE * cycle_size + shard_index) * STRIPE + within % STRIPE


def attend(state, query_block, key_block, value_block, query_pos, query_doc, key_pos, score_scale):
    running_max, running_sum, weighted = state
    scores = (
        jnp.einsum("tkgd,nkd->kgtn", query_block, key_block, preferred_element_type=jnp.float32)
        * score_scale
    )
    visible = (query_doc[:, None] <= key_pos[None, :]) & (key_pos[None, :] <= query_pos[:, None])
    scores = jnp.where(visible, scores, MASKED_SCORE)
    new_max = jnp.maximum(running_max, jnp.max(scores, axis=-1))
    weights = jnp.where(visible, jnp.exp(scores - new_max[..., None]), 0.0).astype(jnp.bfloat16)
    shrink = jnp.exp(running_max - new_max)
    running_sum = running_sum * shrink + jnp.sum(weights.astype(jnp.float32), axis=-1)
    weighted = weighted * shrink[..., None] + jnp.einsum(
        "kgtn,nkd->kgtd", weights, value_block, preferred_element_type=jnp.float32
    )
    return (new_max, running_sum, weighted)


def local(queries, barred_key_rows, barred_value_rows, doc_start, out_weight):
    tok_dev = queries.shape[0]
    key_heads = barred_key_rows.shape[1] // HEAD_SIZE
    heads_per_group = queries.shape[1] // barred_key_rows.shape[1]
    cycle_size = lax.axis_size("ctx")
    score_scale = 1.0 / math.sqrt(HEAD_SIZE)
    own_rows = lax.axis_index("ctx") * tok_dev + jnp.arange(tok_dev, dtype=jnp.int32)
    query_pos = positions(own_rows, tok_dev, cycle_size)
    query_split = queries.reshape(tok_dev, key_heads, heads_per_group, HEAD_SIZE)
    start_state = (
        jnp.full((key_heads, heads_per_group, tok_dev), MASKED_SCORE, jnp.float32),
        jnp.zeros((key_heads, heads_per_group, tok_dev), jnp.float32),
        jnp.zeros((key_heads, heads_per_group, tok_dev, HEAD_SIZE), jnp.float32),
    )
    state = start_state
    key_piece = lax.all_gather(barred_key_rows, "ctx", axis=0, tiled=True)
    value_piece = lax.all_gather(barred_value_rows, "ctx", axis=0, tiled=True)
    fetched_rows = key_piece.shape[0]
    shards = fetched_rows // tok_dev
    per_block = 4
    block_count = shards // per_block
    row_index = jnp.arange(fetched_rows, dtype=jnp.int32)
    key_pos_all = positions(row_index, tok_dev, cycle_size)
    key_blocks = key_piece.reshape(block_count, per_block * tok_dev, key_heads, HEAD_SIZE)
    value_blocks = value_piece.reshape(block_count, per_block * tok_dev, key_heads, HEAD_SIZE)
    pos_blocks = key_pos_all.reshape(block_count, per_block * tok_dev)

    def one_block(carried, block_data):
        key_block, value_block, pos_block = block_data
        return (
            attend(
                carried,
                query_split,
                key_block,
                value_block,
                query_pos,
                doc_start,
                pos_block,
                score_scale,
            ),
            None,
        )

    state, unused = lax.scan(one_block, state, (key_blocks, value_blocks, pos_blocks))
    running_max, running_sum, weighted = state
    scaled = weighted / running_sum[..., None]
    attn = (
        jnp.transpose(scaled, (2, 0, 1, 3))
        .reshape(tok_dev, key_heads * heads_per_group * HEAD_SIZE)
        .astype(jnp.bfloat16)
    )
    partial_out = jnp.dot(attn, out_weight, preferred_element_type=jnp.float32)
    return lax.psum_scatter(
        partial_out.astype(jnp.bfloat16), "head", scatter_dimension=1, tiled=True
    )


def solution(mesh):
    placed = (P("ctx", "head"), P("ctx", "head"), P("ctx", "head"), P("ctx"), P("head", None))
    return jax.shard_map(
        local, mesh=mesh, in_specs=placed, out_specs=P("ctx", "head"), check_vma=False
    )
```

profile of v0, /device:TPU:1, one launch (start us, length us, event | category | flops | bytes accessed | tf_op | source)
XLA Modules:
  0.0 621.1 jit_solution(1597774503833811170)
XLA Ops:
  9.5 223.9 %all-gather.3.cloned.1.call-done = bf16[16384,256]{1,0:T(8,128)(2,1)} async-done(((bf16[128,256]{1,0:T(8,128)(2,1)}), bf16[16384,256]{1,0:T(8,128)(2,1)}) %all-gather.3.cloned.1.call-update) | async-done | bytes 8388624 | tf_op jit(solution)/shard_map/all_gather | solution.py:51
  233.4 12.5 %reshape.30 = bf16[32,512,2,128]{3,2,1,0:T(2,128)(2,1)} reshape(bf16[16384,256]{1,0:T(8,128)(2,1)} %all-gather.3.cloned.1.call-done) | data formatting | bytes 16777216 | tf_op jit(solution)/shard_map/reshape | solution.py:59
  246.0 208.7 %all-gather.5.cloned.1.call-done = bf16[16384,256]{1,0:T(8,128)(2,1)} async-done(((bf16[128,256]{1,0:T(8,128)(2,1)}), bf16[16384,256]{1,0:T(8,128)(2,1)}) %all-gather.5.cloned.1.call-update) | async-done | bytes 8388624 | tf_op jit(solution)/shard_map/all_gather | solution.py:52
  454.6 12.5 %reshape.31 = bf16[32,512,2,128]{3,2,1,0:T(2,128)(2,1)} reshape(bf16[16384,256]{1,0:T(8,128)(2,1)} %all-gather.5.cloned.1.call-done) | data formatting | bytes 16777216 | tf_op jit(solution)/shard_map/reshape | solution.py:60
  467.2 115.4 %while.15 = (s32[]{:T(128)}, f32[2,4,128]{2,1,0:T(4,128)S(1)}, f32[2,4,128]{2,1,0:T(4,128)S(1)}, f32[2,4,128,128]{3,2,1,0:T(8,128)S(1)}, s32[128]{0:T(128)S(1)},...) while((s32[]{:T(128)}, f32[2,4,128]{2,1,0:T(4,128)S(1)}, ...), condition=%wide.region_3.4_spmd.clone, body=%wide.region_0.3_spmd.clone.sunk | while | flops 276900224 | bytes 9510541 | solution.py:79
  467.3 1.4 constant_dynamic-slice_fusion.6
  470.9 1.4 constant_dynamic-slice_fusion.6
  474.6 1.4 constant_dynamic-slice_fusion.6
  478.2 1.4 constant_dynamic-slice_fusion.6
  481.8 1.4 constant_dynamic-slice_fusion.6
  485.4 1.4 constant_dynamic-slice_fusion.6
  489.0 1.4 constant_dynamic-slice_fusion.6
  492.6 1.4 constant_dynamic-slice_fusion.6
  496.2 1.4 constant_dynamic-slice_fusion.6
  499.8 1.4 constant_dynamic-slice_fusion.6
  503.4 1.4 constant_dynamic-slice_fusion.6
  507.0 1.4 constant_dynamic-slice_fusion.6
  510.6 1.4 constant_dynamic-slice_fusion.6
  514.2 1.4 constant_dynamic-slice_fusion.6
  517.8 1.4 constant_dynamic-slice_fusion.6
  521.4 1.4 constant_dynamic-slice_fusion.6
  525.0 1.4 constant_dynamic-slice_fusion.6
  528.7 1.4 constant_dynamic-slice_fusion.6
  532.3 1.4 constant_dynamic-slice_fusion.6
  535.9 1.4 constant_dynamic-slice_fusion.6
  539.5 1.4 constant_dynamic-slice_fusion.6
  550.3 1.4 constant_dynamic-slice_fusion.6
  553.9 1.4 constant_dynamic-slice_fusion.6
  557.5 1.4 constant_dynamic-slice_fusion.6
  564.7 1.4 constant_dynamic-slice_fusion.6
  582.8 5.7 convolution_convert_fusion
  588.5 26.0 %reduce-scatter.2.cloned.1.call-done = bf16[128,2048]{1,0:T(8,128)(2,1)} async-done(((bf16[128,4096]{1,0:T(8,128)(2,1)}), bf16[128,2048]{1,0:T(8,128)(2,1)}) %reduce-scatter.2.cloned.1.call-update) | async-done | bytes 524304 | tf_op jit(solution)/shard_map/reduce_scatter | solution.py:88
  (311 shorter events, 81.6 us)
Async XLA Ops:
  6.5 226.9 %all-gather.3.cloned.1.call-start = ((), (), s32[]{:S(2)}) async-start(), calls=%async_computation.1 | async-start | bytes 8454144 | tf_op jit(solution)/shard_map/all_gather | solution.py:51
  7.3 447.4 %all-gather.5.cloned.1.call-start = ((), (), s32[]{:S(2)}) async-start(), calls=%async_computation.2 | async-start | bytes 8454144 | tf_op jit(solution)/shard_map/all_gather | solution.py:52
  8.0 606.5 %reduce-scatter.2.cloned.1.call-start = ((), (), s32[]{:S(2)}) async-start(), calls=%async_computation.3 | async-start | bytes 1572864 | tf_op jit(solution)/shard_map/reduce_scatter | solution.py:88
  246.0 221.2 %copy-start = (s32[128]{0:T(128)S(1)}, s32[128]{0:T(128)}, u32[]{:S(2)}) copy-start(s32[128]{0:T(128)} %param.10) | copy-start | bytes 1540
Sparse Core Ops, SparseCore 0:
  9.2 224.1 all-gather.2
  235.3 219.2 all-gather.4
  588.6 25.8 reduce-scatter.1
where the time goes:
time: 622 us; the launch traced here: 621 us
  waiting for transfers between devices  460 us (74%)
  local copies, waits for them, and re-layouts  71.7 us (12%)
  matrix products  51.2 us (8%)
  other arithmetic  22.9 us (4%)
  between operations  13.2 us (2%)
    all_gather x1, waiting for transfers between devices, local(): key_piece = lax.all_gather(barred_key_rows, 'ctx', axis=0, tiled=True)  224 us
    all_gather x1, waiting for transfers between devices, local(): value_piece = lax.all_gather(barred_value_rows, 'ctx', axis=0, tiled=True)  209 us
    dynamic_slice x64, local copies, waits for them, and re-layouts, local(): lax.scan(one_block, state, (key_blocks, value_blocks, pos_blocks))  45 us
    dot_general x32, matrix products, attend(): jnp.einsum('kgtn,nkd->kgtd', weights, value_block, preferred_element_type...  30.7 us
    reduce_scatter x1, waiting for transfers between devices, local(): lax.psum_scatter(partial_out.astype(jnp.bfloat16), 'head', scatter_dimens...  26 us
    reduce_sum x32, other arithmetic, attend(): jnp.sum(weights.astype(jnp.float32), axis=-1)  16.7 us
    dot_general x32, matrix products, attend(): jnp.einsum('tkgd,nkd->kgtn', query_block, key_block, preferred_element_ty...  14.9 us
    reshape x1, local copies, waits for them, and re-layouts, local(): key_piece.reshape(block_count, per_block * tok_dev, key_heads, HEAD_SIZE)  12.5 us
  transfers between devices with their start and end apart: 3, of which 3 were waited for; matrix products, arithmetic and copies ran while one was open for 2% of the time, Pallas kernels for 0%

commit v1 on v0

--- a/solution.py
+++ b/solution.py
@@ -49,7 +49,9 @@
     )
     state = start_state
     key_piece = lax.all_gather(barred_key_rows, "ctx", axis=0, tiled=True)
-    value_piece = lax.all_gather(barred_value_rows, "ctx", axis=0, tiled=True)
+    value_piece = jnp.concatenate(
+        lax.all_to_all(jnp.stack([barred_value_rows] * lax.axis_size("ctx")), "ctx", 0, 0), axis=0
+    )
     fetched_rows = key_piece.shape[0]
     shards = fetched_rows // tok_dev
     per_block = 4

time: 622 us -> 511 us (0.82)
  waiting for transfers between devices: 460 us -> 276 us
  matrix products: 51.2 us -> 81 us
  local copies, waits for them, and re-layouts: 71.7 us -> 96.9 us
  starting transfers between devices: 0.08 us -> 15.6 us
    all_gather x1 -> x0, waiting for transfers between devices: 209 us -> none  [local(): value_piece = lax.all_gather(barred_value_rows, 'ctx', axis=0, tiled=True)]
    all_to_all x0 -> x1, waiting for transfers between devices: none -> 207 us  [local(): lax.all_to_all(jnp.stack([barred_value_rows] * lax.axis_size('ctx')), 'ct...]
    all_gather x1, waiting for transfers between devices: 224 us -> 35.8 us  [local(): key_piece = lax.all_gather(barred_key_rows, 'ctx', axis=0, tiled=True)]
    dot_general x32, matrix products: 30.7 us -> 60.5 us  [attend(): jnp.einsum('kgtn,nkd->kgtd', weights, value_block, preferred_element_type...]
    another operation x0 -> x2, local copies, waits for them, and re-layouts: none -> 19.3 us  [the longest x1 14 us: local(): value_piece.reshape(block_count, per_block * tok_dev, key_heads, HEAD_SIZE)]
    all_to_all x0 -> x1, starting transfers between devices: none -> 15.4 us  [local(): lax.all_to_all(jnp.stack([barred_value_rows] * lax.axis_size('ctx')), 'ct...]
    unnamed x4 -> x8, local copies, waits for them, and re-layouts: 1.3 us -> 16 us
    reshape x1 -> x0, local copies, waits for them, and re-layouts: 12.5 us -> none  [local(): value_piece.reshape(block_count, per_block * tok_dev, key_heads, HEAD_SIZE)]
  transfers between devices with their start and end apart: 3 -> 3, of which waited for: 3 -> 3; matrix products, arithmetic and copies ran while one was open for 2% -> 8% of each run, Pallas kernels for 0% -> 0%
where the time goes in v1:
time: 511 us; the launch traced here: 508 us
  waiting for transfers between devices  276 us (54%)
  local copies, waits for them, and re-layouts  96.9 us (19%)
  matrix products  81 us (16%)
  other arithmetic  22.9 us (4%)
  starting transfers between devices  15.6 us (3%)
  between operations  13.5 us (3%)
    all_to_all x1, waiting for transfers between devices, local(): lax.all_to_all(jnp.stack([barred_value_rows] * lax.axis_size('ctx')), 'ct...  207 us
    dot_general x32, matrix products, attend(): jnp.einsum('kgtn,nkd->kgtd', weights, value_block, preferred_element_type...  60.5 us
    dynamic_slice x64, local copies, waits for them, and re-layouts, local(): lax.scan(one_block, state, (key_blocks, value_blocks, pos_blocks))  36.7 us
    all_gather x1, waiting for transfers between devices, local(): key_piece = lax.all_gather(barred_key_rows, 'ctx', axis=0, tiled=True)  35.8 us
    reduce_scatter x1, waiting for transfers between devices, local(): lax.psum_scatter(partial_out.astype(jnp.bfloat16), 'head', scatter_dimens...  31.9 us
    reduce_sum x32, other arithmetic, attend(): jnp.sum(weights.astype(jnp.float32), axis=-1)  16.7 us
    unnamed x8, local copies, waits for them, and re-layouts  16 us
    all_to_all x1, starting transfers between devices, local(): lax.all_to_all(jnp.stack([barred_value_rows] * lax.axis_size('ctx')), 'ct...  15.4 us
  transfers between devices with their start and end apart: 3, of which 3 were waited for; matrix products, arithmetic and copies ran while one was open for 8% of the time, Pallas kernels for 0%

profile of v1, /device:TPU:1, one launch (start us, length us, event | category | flops | bytes accessed | tf_op | source)
XLA Modules:
  0.0 507.9 jit_solution(9622242502170716176)
XLA Ops:
  7.5 5.3 %stack.2 = bf16[128,128,256]{1,2,0:T(8,128)(2,1)} broadcast(bf16[128,256]{0,1:T(8,128)(2,1)S(1)} %copy.18), dimensions={1,2} | broadcast | bytes 8454144 | tf_op jit(solution)/shard_map/stack | solution.py:53
  12.8 15.4 %all-to-all-start = ((bf16[128,128,256]{1,2,0:T(8,128)(2,1)}), bf16[128,128,256]{1,2,0:T(8,128)(2,1)}, u32[]{:S(2)}, u32[]{:S(2)}) async-start(bf16[128,128,256]{1,2,0:T(8,128)(2,1)} %stack.2), calls=%async_computation | async-start | bytes 16777216 | tf_op jit(solution)/shard_map/all_to_all | solution.py:53
  29.7 207.4 %all-to-all-done = bf16[128,128,256]{1,2,0:T(8,128)(2,1)} async-done(((bf16[128,128,256]{1,2,0:T(8,128)(2,1)}), bf16[128,128,256]{1,2,0:T(8,128)(2,1)}, u32[]{:S(2)}, u32[]{:S(2)}) %all-to-all-start) | async-done | bytes 8388640 | tf_op jit(solution)/shard_map/all_to_all | solution.py:53
  237.1 12.0 %copy.19 = bf16[128,128,256]{1,0,2:T(8,128)(2,1)} copy(bf16[128,128,256]{1,2,0:T(8,128)(2,1)} %all-to-all-done) | data formatting | bytes 16777216 | tf_op jit(solution)/shard_map/all_to_all | solution.py:53
  249.1 14.0 %reshape_reshape.3 = bf16[32,512,2,128]{1,0,3,2:T(8,128)(2,1)} reshape(bf16[128,128,256]{1,0,2:T(8,128)(2,1)} %copy.19) | data formatting | bytes 16777216 | tf_op jit(solution)/shard_map/reshape;reshape | solution.py:62
  263.1 14.7 %copy.22 = bf16[32,512,2,128]{3,1,2,0:T(8,128)(2,1)} copy(bf16[32,512,2,128]{1,0,3,2:T(8,128)(2,1)} %reshape_reshape.3) | data formatting | bytes 16777216
  277.8 35.8 %all-gather.2.cloned.1.call-done = bf16[16384,256]{1,0:T(8,128)(2,1)} async-done(((bf16[128,256]{1,0:T(8,128)(2,1)}), bf16[16384,256]{1,0:T(8,128)(2,1)}) %all-gather.2.cloned.1.call-update) | async-done | bytes 8388624 | tf_op jit(solution)/shard_map/all_gather | solution.py:51
  313.6 12.6 %reshape.28 = bf16[32,512,2,128]{3,2,1,0:T(2,128)(2,1)} reshape(bf16[16384,256]{1,0:T(8,128)(2,1)} %all-gather.2.cloned.1.call-done) | data formatting | bytes 16777216 | tf_op jit(solution)/shard_map/reshape | solution.py:61
  326.2 137.0 %while.15 = (s32[]{:T(128)}, f32[2,4,128]{2,1,0:T(4,128)S(1)}, f32[2,4,128]{2,1,0:T(4,128)S(1)}, f32[2,4,128,128]{3,2,1,0:T(8,128)S(1)}, s32[128]{0:T(128)S(1)},...) while((s32[]{:T(128)}, f32[2,4,128]{2,1,0:T(4,128)S(1)}, ...), condition=%wide.region_3.4_spmd.clone, body=%wide.region_0.3_spmd.clone.sunk | while | flops 276900224 | bytes 8986765 | solution.py:81
  328.5 1.9 convolution_add_fusion.2
  332.8 1.9 convolution_add_fusion.2
  337.1 1.9 convolution_add_fusion.2
  341.4 1.9 convolution_add_fusion.2
  345.6 1.9 convolution_add_fusion.2
  349.9 1.9 convolution_add_fusion.2
  354.2 1.9 convolution_add_fusion.2
  358.5 1.9 convolution_add_fusion.2
  362.8 1.9 convolution_add_fusion.2
  367.1 1.9 convolution_add_fusion.2
  375.6 1.9 convolution_add_fusion.2
  384.2 1.9 convolution_add_fusion.2
  392.7 1.9 convolution_add_fusion.2
  401.3 1.9 convolution_add_fusion.2
  409.9 1.9 convolution_add_fusion.2
  418.4 1.9 convolution_add_fusion.2
  427.0 1.9 convolution_add_fusion.2
  435.6 1.9 convolution_add_fusion.2
  444.1 1.9 convolution_add_fusion.2
  452.7 1.9 convolution_add_fusion.2
  461.3 1.9 convolution_add_fusion.2
  463.4 5.6 %convolution_convert_fusion = bf16[128,4096]{1,0:T(8,128)(2,1)} fusion(bf16[128,1024]{0,1:T(8,128)(2,1)S(1)} %bitcast.47, bf16[1024,4096]{1,0:T(8,128)(2,1)} %param.11), kind=kOutput, calls=%fused_computation.30 | convolution fusion | flops 1074266112 | bytes 9699328 | tf_op jit(solution)/shard_map/dot_general | solution.py:89
  469.1 31.9 %reduce-scatter.2.cloned.1.call-done = bf16[128,2048]{1,0:T(8,128)(2,1)} async-done(((bf16[128,4096]{1,0:T(8,128)(2,1)}), bf16[128,2048]{1,0:T(8,128)(2,1)}) %reduce-scatter.2.cloned.1.call-update) | async-done | bytes 524304 | tf_op jit(solution)/shard_map/reduce_scatter | solution.py:90
  (316 shorter events, 97.8 us)
Async XLA Ops:
  12.8 16.4 %copy-start = (bf16[128,1024]{1,0:T(8,128)(2,1)S(1)}, bf16[128,1024]{1,0:T(8,128)(2,1)}, u32[]{:S(2)}) copy-start(bf16[128,1024]{1,0:T(8,128)(2,1)} %param.7) | copy-start | bytes 786436
  12.8 224.3 %all-to-all-start = ((bf16[128,128,256]{1,2,0:T(8,128)(2,1)}), bf16[128,128,256]{1,2,0:T(8,128)(2,1)}, u32[]{:S(2)}, u32[]{:S(2)}) async-start(bf16[128,128,256]{1,2,0:T(8,128)(2,1)} %stack.2), calls=%async_computation | async-start | bytes 16777216 | tf_op jit(solution)/shard_map/all_to_all | solution.py:53
  28.2 285.4 %all-gather.2.cloned.1.call-start = ((), (), s32[]{:S(2)}) async-start(), calls=%async_computation.2 | async-start | bytes 8454144 | tf_op jit(solution)/shard_map/all_gather | solution.py:51
  28.9 472.1 %reduce-scatter.2.cloned.1.call-start = ((), (), s32[]{:S(2)}) async-start(), calls=%async_computation.3 | async-start | bytes 1572864 | tf_op jit(solution)/shard_map/reduce_scatter | solution.py:90
  277.8 48.3 %copy-start.1 = (s32[128]{0:T(128)S(1)}, s32[128]{0:T(128)}, u32[]{:S(2)}) copy-start(s32[128]{0:T(128)} %param.10) | copy-start | bytes 1540
Sparse Core Ops, SparseCore 0:
  30.9 282.6 all-gather.1
  469.2 31.7 reduce-scatter.1
